TPU v7x, 32 devices: a whole 2x2x4 slice. The times are simulated.
32 devices in a mesh: inb: 4 (over y, x), outb: 8 (over z, core).
Axes of the slice: x: 2, y: 2, z: 4, core: 2. Of those that a mesh axis runs over, the one named last changes fastest.
Arguments:
- site_cores: float32 [2, 4, 8192, 8192], P(None, None, 'inb', 'outb')
- left_env: float32 [512, 8192], P(None, 'outb')
- outcomes: int32 [2, 512], replicated, may hold values from 0 to 3
Outputs:
- env_out: float32 [512, 8192], P('inb', 'outb')
- probabilities: float32 [2, 4, 512], P(None, None, 'inb')
- log_scale: float32 [512], P('inb')
All inputs are finite; a program needn't handle non-finite values.
Results may differ from a plain program's by a relative error of at most 0.00014.
Values sent between devices are 32-bit elements; how exact they have to be, the bound alone decides.
A program may use at most 128 MiB of HBM per device.

v0:
```python
import jax
import jax.numpy as jnp
from jax import lax
from jax.sharding import PartitionSpec as P

epsilon = 1e-06


def on_device(site_cores, left_env, outcomes):
    inb_index = lax.axis_index("inb")
    inb_count = lax.axis_size("inb")
    samples_all = left_env.shape[0]
    block_rows = samples_all // inb_count
    width_out = site_cores.shape[3]
    bond_width = width_out * lax.axis_size("outb")
    outcome_count = site_cores.shape[1]
    levels = jnp.arange(outcome_count, dtype=jnp.int32)
    current = lax.dynamic_slice_in_dim(left_env, inb_index * block_rows, block_rows, 0)
    chosen_ids = lax.dynamic_slice_in_dim(outcomes, inb_index * block_rows, block_rows, 1)
    log_scale = jnp.zeros((chosen_ids.shape[1],), jnp.float32)
    prob_list = []
    for site_index in range(site_cores.shape[0]):
        sample_rows = lax.all_gather(current, "outb", axis=1, tiled=True)
        own_cols = lax.all_to_all(sample_rows, "inb", split_axis=1, concat_axis=0, tiled=True)
        partial_terms = jnp.einsum(
            "sc,pcd->psd", own_cols, site_cores[site_index], precision=lax.Precision.HIGHEST
        )
        candidates = lax.psum_scatter(partial_terms, "inb", scatter_dimension=1, tiled=True)
        squares = jnp.sum(candidates * candidates, axis=2)
        totals = lax.psum(squares, "outb")
        mean_squares = totals / bond_width + epsilon
        prob_list.append(mean_squares / jnp.sum(mean_squares, axis=0, keepdims=True))
        onehot = (chosen_ids[site_index][None, :] == levels[:, None]).astype(jnp.float32)
        chosen = jnp.sum(onehot[:, :, None] * candidates, axis=0)
        chosen_mean = jnp.sum(onehot * mean_squares, axis=0)
        inverse = lax.rsqrt(chosen_mean)
        log_scale = log_scale + 0.5 * jnp.log(chosen_mean)
        current = chosen * inverse[:, None]
    prob_stack = jnp.stack(prob_list)
    return (current, prob_stack, log_scale)


def solution(mesh):
    in_specs = (P(None, None, "inb", "outb"), P(None, "outb"), P())
    out_specs = (P("inb", "outb"), P(None, None, "inb"), P("inb"))
    return jax.shard_map(
        on_device, mesh=mesh, in_specs=in_specs, out_specs=out_specs, check_vma=False
    )
```

profile of v0, /device:TPU:0, one launch (start us, length us, event | category | flops | bytes accessed | tf_op | source)
XLA Modules:
  0.0 555.6 jit_solution(1600820002237552070)
XLA Ops:
  7.2 1.5 copy-done
  8.8 0.8 constant_dynamic-slice_fusion
  9.6 0.0 reduce-scatter.3.cloned.1.call-start
  9.7 50.1 %all-gather.3.cloned.1.call-done = f32[128,8192]{1,0:T(8,128)} async-done(((f32[128,1024]{1,0:T(8,128)}), f32[128,8192]{1,0:T(8,128)}) %all-gather.3.cloned.1.call-update) | async-done | bytes 4194320 | tf_op jit(solution)/shard_map/all_gather | solution.py:23
  59.8 2.5 copy.14
  62.3 51.7 %all_to_all.38 = f32[128,4,2048]{2,0,1:T(8,128)S(1)} all-to-all(f32[128,4,2048]{2,0,1:T(8,128)S(1)} %bitcast.46), channel_id=1, replica_groups=mesh['inb'=4,'outb'=8] {'inb'}, dimensions={1} | all-to-all | bytes 8388608 | tf_op jit(solution)/shard_map/all_to_all | solution.py:24
  113.9 59.2 %fusion.6 = f32[4,512,1024]{2,1,0:T(8,128)} fusion(f32[512,2048,1]{1,0,2:T(8,128)S(1)} %bitcast.50, f32[2,4,2048,1024]{3,2,1,0:T(8,128)} %param.3), kind=kOutput, calls=%fused_computation.7 | convolution fusion | flops 51539607552 | bytes 46137344 | tf_op jit(solution)/shard_map/sc,pcd->psd/dot_general | solution.py:25
  173.2 0.2 all-gather.5.cloned.1.call-start
  173.4 0.7 constant_dynamic-slice_fusion.1
  174.1 82.9 %reduce-scatter.3.cloned.1.call-done = f32[4,128,1024]{2,1,0:T(8,128)} async-done(((f32[4,512,1024]{2,1,0:T(8,128)}), f32[4,128,1024]{2,1,0:T(8,128)}) %reduce-scatter.3.cloned.1.call-update) | async-done | bytes 2097168 | tf_op jit(solution)/shard_map/reduce_scatter | solution.py:28
  257.0 2.0 multiply_reduce_fusion.2
  259.0 16.2 %psum.14 = f32[4,128]{1,0:T(4,128)S(1)} all-reduce(f32[4,128]{1,0:T(4,128)S(1)} %get-tuple-element.5), channel_id=1, replica_groups=mesh['inb'=4,'outb'=8] {'outb'}, use_global_device_ids=true, to_apply=%region_3.0 | all-reduce | flops 512 | bytes 4096 | tf_op jit(solution)/shard_map/psum | solution.py:30
  275.2 0.9 broadcast_multiply_fusion.1
  276.2 44.2 %all-gather.5.cloned.1.call-done = f32[128,8192]{1,0:T(8,128)} async-done(((f32[128,1024]{1,0:T(8,128)}), f32[128,8192]{1,0:T(8,128)}) %all-gather.5.cloned.1.call-update) | async-done | bytes 4194320 | tf_op jit(solution)/shard_map/all_gather | solution.py:23
  320.4 5.6 %copy.10 = f32[128,8192]{0,1:T(8,128)} copy(f32[128,8192]{1,0:T(8,128)} %all-gather.5.cloned.1.call-done) | data formatting | bytes 8388608 | tf_op jit(solution)/shard_map/all_gather | solution.py:23
  326.0 54.2 %all_to_all.39 = f32[128,4,2048]{0,2,1:T(8,128)} all-to-all(f32[128,4,2048]{0,2,1:T(8,128)} %bitcast.47), channel_id=1, replica_groups=mesh['inb'=4,'outb'=8] {'inb'}, dimensions={1} | all-to-all | bytes 8388608 | tf_op jit(solution)/shard_map/all_to_all | solution.py:24
  380.2 5.4 copy.11
  385.6 59.2 %fusion.9 = f32[4,512,1024]{2,1,0:T(8,128)} fusion(f32[512,2048,1]{1,0,2:T(8,128)} %bitcast.51, f32[2,4,2048,1024]{3,2,1,0:T(8,128)} %param.3), kind=kOutput, calls=%fused_computation.8 | convolution fusion | flops 51539607552 | bytes 46137344 | tf_op jit(solution)/shard_map/sc,pcd->psd/dot_general | solution.py:25
  444.9 83.9 %reduce-scatter.5.cloned.1.call-done = f32[4,128,1024]{2,1,0:T(8,128)} async-done(((f32[4,512,1024]{2,1,0:T(8,128)}), f32[4,128,1024]{2,1,0:T(8,128)}) %reduce-scatter.5.cloned.1.call-update) | async-done | bytes 2097168 | tf_op jit(solution)/shard_map/reduce_scatter | solution.py:28
  528.8 2.0 multiply_reduce_fusion
  530.8 16.2 %psum.15 = f32[4,128]{1,0:T(4,128)S(1)} all-reduce(f32[4,128]{1,0:T(4,128)S(1)} %get-tuple-element.3), channel_id=1, replica_groups=mesh['inb'=4,'outb'=8] {'outb'}, use_global_device_ids=true, to_apply=%region_8.0 | all-reduce | flops 512 | bytes 4096 | tf_op jit(solution)/shard_map/psum | solution.py:30
  547.1 0.5 add_multiply_fusion
  547.6 0.6 pad_maximum_fusion
  548.2 0.9 broadcast_multiply_fusion
  (15 shorter events, 0.2 us)
Async XLA Ops:
  7.2 1.6 copy-start
  7.2 52.6 %all-gather.3.cloned.1.call-start = ((), (), s32[]{:S(2)}) async-start(), calls=%async_computation.4 | async-start | bytes 4718592 | tf_op jit(solution)/shard_map/all_gather | solution.py:23
  9.6 247.4 %reduce-scatter.3.cloned.1.call-start = ((), (), s32[]{:S(2)}) async-start(), calls=%async_computation.5 | async-start | bytes 10485760 | tf_op jit(solution)/shard_map/reduce_scatter | solution.py:28
  173.2 147.2 %all-gather.5.cloned.1.call-start = ((), (), s32[]{:S(2)}) async-start(), calls=%async_computation.6 | async-start | bytes 4718592 | tf_op jit(solution)/shard_map/all_gather | solution.py:23
  276.1 252.7 %reduce-scatter.5.cloned.1.call-start = ((), (), s32[]{:S(2)}) async-start(), calls=%async_computation.7 | async-start | bytes 10485760 | tf_op jit(solution)/shard_map/reduce_scatter | solution.py:28
Sparse Core Ops, SparseCore 0:
  10.2 49.5 all-gather.2
  173.3 83.6 reduce-scatter.2
  276.3 44.0 all-gather.4
  445.0 83.7 reduce-scatter.4
where the time goes:
time: 556 us
  waiting for transfers between devices  261 us (47%)
  blocking collectives  138 us (25%)
  matrix products  118 us (21%)
  local copies, waits for them, and re-layouts  16.5 us (3%)
  between operations  13.8 us (2%)
  other arithmetic  6.98 us (1%)
    reduce_scatter x2, waiting for transfers between devices, on_device(): lax.psum_scatter(partial_terms, 'inb', scatter_dimension=1, tiled=True)  167 us
    dot_general x2, matrix products, on_device(): jnp.einsum('sc,pcd->psd', own_cols, site_cores[site_index], precision=lax...  118 us
    all_to_all x2, blocking collectives, on_device(): lax.all_to_all(sample_rows, 'inb', split_axis=1, concat_axis=0, tiled=True)  106 us
    all_gather x2, waiting for transfers between devices, on_device(): sample_rows = lax.all_gather(current, 'outb', axis=1, tiled=True)  94.3 us
    psum x2, blocking collectives, on_device(): totals = lax.psum(squares, 'outb')  32.4 us
  transfers between devices with their start and end apart: 4, of which 4 were waited for; matrix products, arithmetic and copies ran while one was open for 0% of the time, Pallas kernels for 0%

commit v1 on v0

--- a/solution.py
+++ b/solution.py
@@ -20,7 +20,17 @@
     log_scale = jnp.zeros((chosen_ids.shape[1],), jnp.float32)
     prob_list = []
     for site_index in range(site_cores.shape[0]):
-        sample_rows = lax.all_gather(current, "outb", axis=1, tiled=True)
+        x = current
+        ways, here, step = (lax.axis_size("outb"), lax.axis_index("outb"), x.shape[1])
+        shape = [n * ways if d == 1 else n for d, n in enumerate(x.shape)]
+        sample_rows = lax.dynamic_update_slice_in_dim(
+            jnp.zeros(shape, x.dtype), x, here * step, axis=1
+        )
+        for far in range(1, ways):
+            x = lax.ppermute(x, "outb", [(d, (d + 1) % ways) for d in range(ways)])
+            sample_rows = lax.dynamic_update_slice_in_dim(
+                sample_rows, x, (here - far) % ways * step, axis=1
+            )
         own_cols = lax.all_to_all(sample_rows, "inb", split_axis=1, concat_axis=0, tiled=True)
         partial_terms = jnp.einsum(
             "sc,pcd->psd", own_cols, site_cores[site_index], precision=lax.Precision.HIGHEST

time: 556 us -> 597 us (1.074)
  waiting for transfers between devices: 261 us -> 298 us
  local copies, waits for them, and re-layouts: 16.5 us -> 36.5 us
  blocking collectives: 138 us -> 122 us
    ppermute x0 -> x14, waiting for transfers between devices: none -> 127 us  [on_device(): x = lax.ppermute(x, 'outb', [(d, (d + 1) % ways) for d in range(ways)])]
    all_gather x2 -> x0, waiting for transfers between devices: 94.3 us -> none  [on_device(): sample_rows = lax.all_gather(current, 'outb', axis=1, tiled=True)]
    all_to_all x2, blocking collectives: 106 us -> 89.1 us  [on_device(): lax.all_to_all(sample_rows, 'inb', split_axis=1, concat_axis=0, tiled=True)]
    dynamic_update_slice x0 -> x16, local copies, waits for them, and re-layouts: none -> 9.18 us  [the longest x14 8.31 us: on_device(): lax.dynamic_update_slice_in_dim(sample_rows, x, (here - far) % ways * ste...]
    ppermute x0 -> x7, local copies, waits for them, and re-layouts: none -> 7.57 us  [on_device(): x = lax.ppermute(x, 'outb', [(d, (d + 1) % ways) for d in range(ways)])]
  transfers between devices with their start and end apart: 4 -> 16, of which waited for: 4 -> 16; matrix products, arithmetic and copies ran while one was open for 0% -> 3% of each run, Pallas kernels for 0% -> 0%
where the time goes in v1:
time: 597 us; the launch traced here: 596 us
  waiting for transfers between devices  298 us (50%)
  blocking collectives  122 us (20%)
  matrix products  119 us (20%)
  local copies, waits for them, and re-layouts  36.5 us (6%)
  between operations  14.3 us (2%)
  other arithmetic  6.19 us (1%)
    reduce_scatter x2, waiting for transfers between devices, on_device(): lax.psum_scatter(partial_terms, 'inb', scatter_dimension=1, tiled=True)  171 us
    ppermute x14, waiting for transfers between devices, on_device(): x = lax.ppermute(x, 'outb', [(d, (d + 1) % ways) for d in range(ways)])  127 us
    dot_general x2, matrix products, on_device(): jnp.einsum('sc,pcd->psd', own_cols, site_cores[site_index], precision=lax...  119 us
    all_to_all x2, blocking collectives, on_device(): lax.all_to_all(sample_rows, 'inb', split_axis=1, concat_axis=0, tiled=True)  89.1 us
    psum x2, blocking collectives, on_device(): totals = lax.psum(squares, 'outb')  32.4 us
  transfers between devices with their start and end apart: 16, of which 16 were waited for; matrix products, arithmetic and copies ran while one was open for 3% of the time, Pallas kernels for 0%

profile of v1, /device:TPU:0, one launch (start us, length us, event | category | flops | bytes accessed | tf_op | source)
XLA Modules:
  0.0 596.0 jit_solution(8416400622129177261)
XLA Ops:
  9.5 10.9 %collective-permute-done = f32[128,1024]{0,1:T(8,128)S(1)} collective-permute-done((f32[128,1024]{0,1:T(8,128)S(1)}, f32[128,1024]{0,1:T(8,128)S(1)}, u32[]{:S(2)}, u32[]{:S(2)}) %collective-permute-start) | collective-permute-done | bytes 524320 | tf_op jit(solution)/shard_map/ppermute | solution.py:30
  20.4 10.4 %collective-permute-done.1 = f32[128,1024]{0,1:T(8,128)S(1)} collective-permute-done((f32[128,1024]{0,1:T(8,128)S(1)}, f32[128,1024]{0,1:T(8,128)S(1)}, u32[]{:S(2)}, u32[]{:S(2)}) %collective-permute-start.1) | collective-permute-done | bytes 524320 | tf_op jit(solution)/shard_map/ppermute | solution.py:30
  30.8 10.4 %collective-permute-done.2 = f32[128,1024]{0,1:T(8,128)S(1)} collective-permute-done((f32[128,1024]{0,1:T(8,128)S(1)}, f32[128,1024]{0,1:T(8,128)S(1)}, u32[]{:S(2)}, u32[]{:S(2)}) %collective-permute-start.2) | collective-permute-done | bytes 524320 | tf_op jit(solution)/shard_map/ppermute | solution.py:30
  42.0 9.6 %collective-permute-done.3 = f32[128,1024]{0,1:T(8,128)S(1)} collective-permute-done((f32[128,1024]{0,1:T(8,128)S(1)}, f32[128,1024]{0,1:T(8,128)S(1)}, u32[]{:S(2)}, u32[]{:S(2)}) %collective-permute-start.3) | collective-permute-done | bytes 524320 | tf_op jit(solution)/shard_map/ppermute | solution.py:30
  52.5 10.5 %collective-permute-done.4 = f32[128,1024]{0,1:T(8,128)} collective-permute-done((f32[128,1024]{0,1:T(8,128)S(1)}, f32[128,1024]{0,1:T(8,128)}, u32[]{:S(2)}, u32[]{:S(2)}) %collective-permute-start.4) | collective-permute-done | bytes 524320 | tf_op jit(solution)/shard_map/ppermute | solution.py:30
  64.0 9.6 %collective-permute-done.5 = f32[128,1024]{0,1:T(8,128)} collective-permute-done((f32[128,1024]{0,1:T(8,128)}, f32[128,1024]{0,1:T(8,128)}, u32[]{:S(2)}, u32[]{:S(2)}) %collective-permute-start.5) | collective-permute-done | bytes 524320 | tf_op jit(solution)/shard_map/ppermute | solution.py:30
  76.0 8.3 %collective-permute-done.6 = f32[128,1024]{0,1:T(8,128)S(1)} collective-permute-done((f32[128,1024]{0,1:T(8,128)}, f32[128,1024]{0,1:T(8,128)S(1)}, u32[]{:S(2)}, u32[]{:S(2)}) %collective-permute-start.6) | collective-permute-done | bytes 524320 | tf_op jit(solution)/shard_map/ppermute | solution.py:30
  84.3 43.6 %all_to_all.38 = f32[128,4,2048]{0,2,1:T(8,128)} all-to-all(f32[128,4,2048]{0,2,1:T(8,128)S(1)} %bitcast.42), channel_id=1, replica_groups=mesh['inb'=4,'outb'=8] {'inb'}, dimensions={1} | all-to-all | bytes 8388608 | tf_op jit(solution)/shard_map/all_to_all | solution.py:34
  128.0 5.4 copy.10
  133.3 59.3 %fusion.6 = f32[4,512,1024]{2,1,0:T(8,128)} fusion(f32[512,2048,1]{1,0,2:T(8,128)} %bitcast.45, f32[2,4,2048,1024]{3,2,1,0:T(8,128)} %param.3), kind=kOutput, calls=%fused_computation.6 | convolution fusion | flops 51539607552 | bytes 46137344 | tf_op jit(solution)/shard_map/sc,pcd->psd/dot_general | solution.py:35
  193.4 82.4 %reduce-scatter.3.cloned.1.call-done = f32[4,128,1024]{2,1,0:T(8,128)} async-done(((f32[4,512,1024]{2,1,0:T(8,128)}), f32[4,128,1024]{2,1,0:T(8,128)}) %reduce-scatter.3.cloned.1.call-update) | async-done | bytes 2097168 | tf_op jit(solution)/shard_map/reduce_scatter | solution.py:38
  277.9 16.2 %psum.14 = f32[4,128]{1,0:T(4,128)S(1)} all-reduce(f32[4,128]{1,0:T(4,128)S(1)} %get-tuple-element.5), channel_id=1, replica_groups=mesh['inb'=4,'outb'=8] {'outb'}, use_global_device_ids=true, to_apply=%region_3.4 | all-reduce | flops 512 | bytes 4096 | tf_op jit(solution)/shard_map/psum | solution.py:40
  294.3 10.4 %collective-permute-done.7 = f32[128,1024]{1,0:T(8,128)S(1)} collective-permute-done((f32[128,1024]{1,0:T(8,128)S(1)}, f32[128,1024]{1,0:T(8,128)S(1)}, u32[]{:S(2)}, u32[]{:S(2)}) %collective-permute-start.7) | collective-permute-done | bytes 524320 | tf_op jit(solution)/shard_map/ppermute | solution.py:30
  305.4 9.6 %collective-permute-done.8 = f32[128,1024]{1,0:T(8,128)S(1)} collective-permute-done((f32[128,1024]{1,0:T(8,128)S(1)}, f32[128,1024]{1,0:T(8,128)S(1)}, u32[]{:S(2)}, u32[]{:S(2)}) %collective-permute-start.8) | collective-permute-done | bytes 524320 | tf_op jit(solution)/shard_map/ppermute | solution.py:30
  315.9 9.6 %collective-permute-done.9 = f32[128,1024]{1,0:T(8,128)S(1)} collective-permute-done((f32[128,1024]{1,0:T(8,128)S(1)}, f32[128,1024]{1,0:T(8,128)S(1)}, u32[]{:S(2)}, u32[]{:S(2)}) %collective-permute-start.9) | collective-permute-done | bytes 524320 | tf_op jit(solution)/shard_map/ppermute | solution.py:30
  325.5 10.4 %collective-permute-done.10 = f32[128,1024]{1,0:T(8,128)S(1)} collective-permute-done((f32[128,1024]{1,0:T(8,128)S(1)}, f32[128,1024]{1,0:T(8,128)S(1)}, u32[]{:S(2)}, u32[]{:S(2)}) %collective-permute-start.10) | collective-permute-done | bytes 524320 | tf_op jit(solution)/shard_map/ppermute | solution.py:30
  335.9 10.5 %collective-permute-done.11 = f32[128,1024]{1,0:T(8,128)} collective-permute-done((f32[128,1024]{1,0:T(8,128)S(1)}, f32[128,1024]{1,0:T(8,128)}, u32[]{:S(2)}, u32[]{:S(2)}) %collective-permute-start.11) | collective-permute-done | bytes 524320 | tf_op jit(solution)/shard_map/ppermute | solution.py:30
  353.0 4.1 collective-permute-done.12
  365.2 2.6 collective-permute-done.13
  369.9 45.5 %all_to_all.39 = f32[128,4,2048]{0,2,1:T(8,128)} all-to-all(f32[128,4,2048]{0,2,1:T(8,128)} %bitcast.8), channel_id=1, replica_groups=mesh['inb'=4,'outb'=8] {'inb'}, dimensions={1} | all-to-all | bytes 8388608 | tf_op jit(solution)/shard_map/all_to_all | solution.py:34
  415.4 5.4 copy.19
  420.8 59.3 %fusion.9 = f32[4,512,1024]{2,1,0:T(8,128)} fusion(f32[512,2048,1]{1,0,2:T(8,128)} %bitcast.46, f32[2,4,2048,1024]{3,2,1,0:T(8,128)} %param.3), kind=kOutput, calls=%fused_computation.7 | convolution fusion | flops 51539607552 | bytes 46137344 | tf_op jit(solution)/shard_map/sc,pcd->psd/dot_general | solution.py:35
  480.1 88.8 %reduce-scatter.5.cloned.1.call-done = f32[4,128,1024]{2,1,0:T(8,128)} async-done(((f32[4,512,1024]{2,1,0:T(8,128)}), f32[4,128,1024]{2,1,0:T(8,128)}) %reduce-scatter.5.cloned.1.call-update) | async-done | bytes 2097168 | tf_op jit(solution)/shard_map/reduce_scatter | solution.py:38
  570.9 16.2 %psum.15 = f32[4,128]{1,0:T(4,128)S(1)} all-reduce(f32[4,128]{1,0:T(4,128)S(1)} %get-tuple-element.3), channel_id=1, replica_groups=mesh['inb'=4,'outb'=8] {'outb'}, use_global_device_ids=true, to_apply=%region_8.9 | all-reduce | flops 512 | bytes 4096 | tf_op jit(solution)/shard_map/psum | solution.py:40
  (85 shorter events, 32.7 us)
Async XLA Ops:
  7.2 1.6 copy-start
  7.2 268.7 %reduce-scatter.3.cloned.1.call-start = ((), (), s32[]{:S(2)}) async-start(), calls=%async_computation.4 | async-start | bytes 10485760 | tf_op jit(solution)/shard_map/reduce_scatter | solution.py:38
  9.0 11.4 %collective-permute-start = (f32[128,1024]{0,1:T(8,128)S(1)}, f32[128,1024]{0,1:T(8,128)S(1)}, u32[]{:S(2)}, u32[]{:S(2)}) collective-permute-start(f32[128,1024]{0,1:T(8,128)S(1)} %copy.20), channel_id=1, source_target_pairs={{0,1},{1,2},{2,3},{3,4},{4,5},{5,6},{6,7},{7,0},{8,9},{9,10},{10,1... | collective-permute-start | bytes 1572872 | tf_op jit(solution)/shard_map/ppermute | solution.py:30
  20.4 20.8 %copy-start.6 = (f32[128,1024]{0,1:T(8,128)}, f32[128,1024]{0,1:T(8,128)S(1)}, u32[]{:S(2)}) copy-start(f32[128,1024]{0,1:T(8,128)S(1)} %collective-permute-done) | copy-start | bytes 1572868
  20.4 10.4 %collective-permute-start.1 = (f32[128,1024]{0,1:T(8,128)S(1)}, f32[128,1024]{0,1:T(8,128)S(1)}, u32[]{:S(2)}, u32[]{:S(2)}) collective-permute-start(f32[128,1024]{0,1:T(8,128)S(1)} %collective-permute-done), channel_id=1, source_target_pairs={{0,1},{1,2},{2,3},{3,4},{4,5},{5,6},{6,7},{7,0},{8,9},{9,10},{10,1... | collective-permute-start | bytes 1572872 | tf_op jit(solution)/shard_map/ppermute | solution.py:30
  30.8 10.4 %collective-permute-start.2 = (f32[128,1024]{0,1:T(8,128)S(1)}, f32[128,1024]{0,1:T(8,128)S(1)}, u32[]{:S(2)}, u32[]{:S(2)}) collective-permute-start(f32[128,1024]{0,1:T(8,128)S(1)} %collective-permute-done.1), channel_id=1, source_target_pairs={{0,1},{1,2},{2,3},{3,4},{4,5},{5,6},{6,7},{7,0},{8,9},{9,10},{10,1... | collective-permute-start | bytes 1572872 | tf_op jit(solution)/shard_map/ppermute | solution.py:30
  41.2 10.4 %collective-permute-start.3 = (f32[128,1024]{0,1:T(8,128)S(1)}, f32[128,1024]{0,1:T(8,128)S(1)}, u32[]{:S(2)}, u32[]{:S(2)}) collective-permute-start(f32[128,1024]{0,1:T(8,128)S(1)} %collective-permute-done.2), channel_id=1, source_target_pairs={{0,1},{1,2},{2,3},{3,4},{4,5},{5,6},{6,7},{7,0},{8,9},{9,10},{10,1... | collective-permute-start | bytes 1572872 | tf_op jit(solution)/shard_map/ppermute | solution.py:30
  52.5 10.5 %collective-permute-start.4 = (f32[128,1024]{0,1:T(8,128)S(1)}, f32[128,1024]{0,1:T(8,128)}, u32[]{:S(2)}, u32[]{:S(2)}) collective-permute-start(f32[128,1024]{0,1:T(8,128)S(1)} %collective-permute-done.3), channel_id=1, source_target_pairs={{0,1},{1,2},{2,3},{3,4},{4,5},{5,6},{6,7},{7,0},{8,9},{9,10},{10,1... | collective-permute-start | bytes 1572872 | tf_op jit(solution)/shard_map/ppermute | solution.py:30
  63.0 10.7 %collective-permute-start.5 = (f32[128,1024]{0,1:T(8,128)}, f32[128,1024]{0,1:T(8,128)}, u32[]{:S(2)}, u32[]{:S(2)}) collective-permute-start(f32[128,1024]{0,1:T(8,128)} %collective-permute-done.4), channel_id=1, source_target_pairs={{0,1},{1,2},{2,3},{3,4},{4,5},{5,6},{6,7},{7,0},{8,9},{9,10},{10,1... | collective-permute-start | bytes 1572872 | tf_op jit(solution)/shard_map/ppermute | solution.py:30
  63.0 1.0 copy-start.7
  63.0 10.8 %copy-start.9 = (f32[128,1024]{0,1:T(8,128)S(1)}, f32[128,1024]{0,1:T(8,128)}, u32[]{:S(2)}) copy-start(f32[128,1024]{0,1:T(8,128)} %copy-done.8) | copy-start | bytes 1572868
  63.0 10.8 %copy-start.11 = (f32[128,1024]{0,1:T(8,128)S(1)}, f32[128,1024]{0,1:T(8,128)}, u32[]{:S(2)}) copy-start(f32[128,1024]{0,1:T(8,128)} %copy-done.10) | copy-start | bytes 1572868
  73.7 10.6 %collective-permute-start.6 = (f32[128,1024]{0,1:T(8,128)}, f32[128,1024]{0,1:T(8,128)S(1)}, u32[]{:S(2)}, u32[]{:S(2)}) collective-permute-start(f32[128,1024]{0,1:T(8,128)} %collective-permute-done.5), channel_id=1, source_target_pairs={{0,1},{1,2},{2,3},{3,4},{4,5},{5,6},{6,7},{7,0},{8,9},{9,10},{10,1... | collective-permute-start | bytes 1572872 | tf_op jit(solution)/shard_map/ppermute | solution.py:30
  192.7 376.3 %reduce-scatter.5.cloned.1.call-start = ((), (), s32[]{:S(2)}) async-start(), calls=%async_computation.5 | async-start | bytes 10485760 | tf_op jit(solution)/shard_map/reduce_scatter | solution.py:38
  294.2 10.5 %collective-permute-start.7 = (f32[128,1024]{1,0:T(8,128)S(1)}, f32[128,1024]{1,0:T(8,128)S(1)}, u32[]{:S(2)}, u32[]{:S(2)}) collective-permute-start(f32[128,1024]{1,0:T(8,128)S(1)} %broadcast_multiply_fusion.1), channel_id=1, source_target_pairs={{0,1},{1,2},{2,3},{3,4},{4,5},{5,6},{6,7},{7,0},{8,9},{9,10},{10,1... | collective-permute-start | bytes 1572872 | tf_op jit(solution)/shard_map/ppermute | solution.py:30
  304.7 10.4 %collective-permute-start.8 = (f32[128,1024]{1,0:T(8,128)S(1)}, f32[128,1024]{1,0:T(8,128)S(1)}, u32[]{:S(2)}, u32[]{:S(2)}) collective-permute-start(f32[128,1024]{1,0:T(8,128)S(1)} %collective-permute-done.7), channel_id=1, source_target_pairs={{0,1},{1,2},{2,3},{3,4},{4,5},{5,6},{6,7},{7,0},{8,9},{9,10},{10,1... | collective-permute-start | bytes 1572872 | tf_op jit(solution)/shard_map/ppermute | solution.py:30
  315.1 10.4 %collective-permute-start.9 = (f32[128,1024]{1,0:T(8,128)S(1)}, f32[128,1024]{1,0:T(8,128)S(1)}, u32[]{:S(2)}, u32[]{:S(2)}) collective-permute-start(f32[128,1024]{1,0:T(8,128)S(1)} %collective-permute-done.8), channel_id=1, source_target_pairs={{0,1},{1,2},{2,3},{3,4},{4,5},{5,6},{6,7},{7,0},{8,9},{9,10},{10,1... | collective-permute-start | bytes 1572872 | tf_op jit(solution)/shard_map/ppermute | solution.py:30
  325.5 20.9 %copy-start.1 = (f32[128,1024]{1,0:T(8,128)}, f32[128,1024]{1,0:T(8,128)S(1)}, u32[]{:S(2)}) copy-start(f32[128,1024]{1,0:T(8,128)S(1)} %collective-permute-done.9) | copy-start | bytes 1572868
  325.5 10.4 %collective-permute-start.10 = (f32[128,1024]{1,0:T(8,128)S(1)}, f32[128,1024]{1,0:T(8,128)S(1)}, u32[]{:S(2)}, u32[]{:S(2)}) collective-permute-start(f32[128,1024]{1,0:T(8,128)S(1)} %collective-permute-done.9), channel_id=1, source_target_pairs={{0,1},{1,2},{2,3},{3,4},{4,5},{5,6},{6,7},{7,0},{8,9},{9,10},{10,1... | collective-permute-start | bytes 1572872 | tf_op jit(solution)/shard_map/ppermute | solution.py:30
  335.9 10.5 %copy-start.3 = (f32[128,1024]{1,0:T(8,128)}, f32[128,1024]{1,0:T(8,128)S(1)}, u32[]{:S(2)}) copy-start(f32[128,1024]{1,0:T(8,128)S(1)} %collective-permute-done.10) | copy-start | bytes 1572868
  335.9 10.5 %collective-permute-start.11 = (f32[128,1024]{1,0:T(8,128)S(1)}, f32[128,1024]{1,0:T(8,128)}, u32[]{:S(2)}, u32[]{:S(2)}) collective-permute-start(f32[128,1024]{1,0:T(8,128)S(1)} %collective-permute-done.10), channel_id=1, source_target_pairs={{0,1},{1,2},{2,3},{3,4},{4,5},{5,6},{6,7},{7,0},{8,9},{9,10},{10,1... | collective-permute-start | bytes 1572872 | tf_op jit(solution)/shard_map/ppermute | solution.py:30
  346.4 10.7 %collective-permute-start.12 = (f32[128,1024]{1,0:T(8,128)}, f32[128,1024]{1,0:T(8,128)}, u32[]{:S(2)}, u32[]{:S(2)}) collective-permute-start(f32[128,1024]{1,0:T(8,128)} %collective-permute-done.11), channel_id=1, source_target_pairs={{0,1},{1,2},{2,3},{3,4},{4,5},{5,6},{6,7},{7,0},{8,9},{9,10},{10,1... | collective-permute-start | bytes 1572872 | tf_op jit(solution)/shard_map/ppermute | solution.py:30
  346.6 11.3 %copy-start.2 = (f32[128,1024]{1,0:T(8,128)S(1)}, f32[128,1024]{1,0:T(8,128)}, u32[]{:S(2)}) copy-start(f32[128,1024]{1,0:T(8,128)} %copy-done.1) | copy-start | bytes 1572868
  357.1 10.7 %collective-permute-start.13 = (f32[128,1024]{1,0:T(8,128)}, f32[128,1024]{1,0:T(8,128)}, u32[]{:S(2)}, u32[]{:S(2)}) collective-permute-start(f32[128,1024]{1,0:T(8,128)} %collective-permute-done.12), channel_id=1, source_target_pairs={{0,1},{1,2},{2,3},{3,4},{4,5},{5,6},{6,7},{7,0},{8,9},{9,10},{10,1... | collective-permute-start | bytes 1572872 | tf_op jit(solution)/shard_map/ppermute | solution.py:30
  (4 other events, 3.2 us)
Sparse Core Ops, SparseCore 0:
  192.8 83.0 reduce-scatter.2
  480.2 88.6 reduce-scatter.4
